TPU v7x, 32 devices: a whole 2x2x4 slice. The times are simulated.
32 devices in a mesh: layer: 4 (over y, x), lat: 8 (over z, core).
Axes of the slice: x: 2, y: 2, z: 4, core: 2. Of those that a mesh axis runs over, the one named last changes fastest.
Arguments:
- inputs: bfloat16 [4, 1, 5120, 128], P(None, None, 'lat'), may hold values from -6 to 6
- encoder: bfloat16 [4, 8192, 5120], P('layer', 'lat'), may hold values from -0.125 to 0.125
- decoder: bfloat16 [4, 4, 8192, 5120], P('layer', None, 'lat'), may hold values from -0.09375 to 0.09375
- encoder_bias: float32 [4, 8192], P(None, 'lat'), may hold values from -3 to 3
- tile_mask: int32 [4, 64, 128], P(None, 'lat'), may hold values 0 or 1
- targets: bfloat16 [1, 5120, 4, 128], P(None, 'lat'), may hold values from -6 to 6
- decoder_bias: float32 [1, 5120, 4], P(None, 'lat'), may hold values from -3 to 3
Outputs:
- errors: bfloat16 [1, 5120, 4, 128], P(None, 'lat')
- input_grads: bfloat16 [4, 5120, 128], P('layer', 'lat')
All inputs are finite; a program needn't handle non-finite values. No bound on the sum of `tile_mask` on one device may be relied on, other than what follows from the above.
Results may differ from a plain program's by a relative error of at most 0.0065.
Values may be sent and summed in bfloat16 or wider, within the bound.
A program may use at most 192 MiB of HBM per device.

v0:
```python
import jax
import jax.numpy as jnp
from jax import lax
from jax.sharding import PartitionSpec as P

TILE = 128


def over_sources(values):
    return lax.psum(values, "layer")


def run_blocks(totals, source_row, blocks, base_target, low_target, high_target, update):

    def advance(target, current):
        weights = lax.dynamic_index_in_dim(blocks, target - base_target, 0, keepdims=False)
        return update(current, target, source_row, weights)

    return lax.fori_loop(low_target, high_target, advance, totals)


def per_device(inputs, encoder, decoder, encoder_bias, tile_mask, targets, decoder_bias):
    layer_count = lax.axis_size("layer")
    lat_count = lax.axis_size("lat")
    layers = decoder.shape[1]
    quarters = layer_count // layers
    position = lax.axis_index("layer")
    source = position // quarters
    quarter = position % quarters
    encoder_rows = encoder[0]
    own_blocks = decoder[0]
    local_latents = encoder_rows.shape[0]
    quarter_width = encoder_rows.shape[1]
    kept_width = quarter_width // lat_count
    row_count = inputs.shape[3]
    block_jobs = [(source, own_blocks, 0, source, layers)]

    def run_all(totals, update):
        block_job = block_jobs[0]
        totals = run_blocks(
            totals, block_job[0], block_job[1], block_job[2], block_job[3], block_job[4], update
        )
        return totals

    own_input = lax.dynamic_index_in_dim(
        inputs.reshape((layers * quarters,) + inputs.shape[2:]), position, 0, keepdims=False
    )
    full_input = lax.all_gather(own_input, "lat", axis=0, tiled=True)
    own_preacts = jnp.dot(encoder_rows, full_input, preferred_element_type=jnp.float32)
    tile_count = tile_mask.shape[1]
    support = jnp.broadcast_to(
        tile_mask[:, :, None, :].astype(jnp.float32), (layers, tile_count, TILE, row_count)
    ).reshape(layers, local_latents, row_count)
    own_support = lax.dynamic_index_in_dim(support, source, 0, keepdims=False)
    source_slots = lax.dynamic_update_index_in_dim(
        jnp.zeros((layers, local_latents, row_count), jnp.float32), own_preacts, source, 0
    )
    preacts = over_sources(source_slots) + encoder_bias[:, :, None]
    activity = (jnp.maximum(preacts, 0.0) * support).astype(jnp.bfloat16)

    def forward_term():

        def update(current, target, source_row, weights):
            latent = lax.dynamic_index_in_dim(activity, source_row, 0, keepdims=False)
            contrib = lax.dot_general(
                weights, latent, (((0,), (0,)), ((), ())), preferred_element_type=jnp.float32
            )
            before = lax.dynamic_index_in_dim(current, target, 1, keepdims=False)
            return lax.dynamic_update_index_in_dim(current, before + contrib, target, 1)

        return run_all(
            jnp.zeros((kept_width * lax.axis_size("lat"), layers, row_count), jnp.float32), update
        )

    partial_value = lax.psum_scatter(forward_term(), "lat", scatter_dimension=0, tiled=True)
    placed = lax.dynamic_update_index_in_dim(
        jnp.zeros((quarters,) + partial_value.shape, jnp.float32), partial_value, quarter, 0
    )
    summed = over_sources(placed)
    errors = (summed + decoder_bias[:, :, :, None] - targets.astype(jnp.float32)).astype(
        jnp.bfloat16
    )
    own_errors = lax.dynamic_index_in_dim(errors, quarter, 0, keepdims=False)

    def fold_errors(totals, portion):

        def update(current, target, source_row, weights):
            error_rows = lax.dynamic_index_in_dim(portion, target, 1, keepdims=False)
            contrib = jnp.dot(weights, error_rows, preferred_element_type=jnp.float32)
            before = lax.dynamic_index_in_dim(current, source_row, 0, keepdims=False)
            return lax.dynamic_update_index_in_dim(current, before + contrib, source_row, 0)

        return run_all(totals, update)

    latent_sums = fold_errors(
        jnp.zeros((layers, local_latents, row_count), jnp.float32),
        lax.all_gather(own_errors, "lat", axis=0, tiled=True),
    )
    latent_grad = over_sources(latent_sums)
    own_latent = lax.dynamic_index_in_dim(latent_grad, source, 0, keepdims=False)
    own_grad = (own_latent * own_support).astype(jnp.bfloat16)
    gradients = lax.psum_scatter(
        lax.dot_general(
            encoder_rows, own_grad, (((0,), (0,)), ((), ())), preferred_element_type=jnp.float32
        ),
        "lat",
        scatter_dimension=0,
        tiled=True,
    )
    return (errors, gradients.astype(jnp.bfloat16)[None])


def solution(mesh):
    in_specs = (
        P(None, None, "lat", None),
        P("layer", "lat", None),
        P("layer", None, "lat", None),
        P(None, "lat"),
        P(None, "lat", None),
        P(None, "lat", None, None),
        P(None, "lat", None),
    )
    out_specs = (P(None, "lat", None, None), P("layer", "lat", None))
    return jax.shard_map(
        per_device, mesh=mesh, in_specs=in_specs, out_specs=out_specs, check_vma=False
    )
```

profile of v0, /device:TPU:0, one launch (start us, length us, event | category | flops | bytes accessed | tf_op | source)
XLA Modules:
  0.0 923.1 jit_solution(17247908552409753957)
XLA Ops:
  9.0 27.4 %all-gather.5.cloned.1.call-done = bf16[1,1,5120,128]{3,2,1,0:T(8,128)(2,1)} async-done(((bf16[1,1,640,128]{3,2,1,0:T(8,128)(2,1)}), bf16[1,1,5120,128]{3,2,1,0:T(8,128)(2,1)}) %all-gather.5.cloned.1.call-update) | async-done | bytes 1310736 | tf_op jit(solution)/shard_map/all_gather | solution.py:48
  36.4 8.0 fusion.37
  46.9 68.4 %all-reduce.6.cloned.1.call-done = f32[4,1024,128]{2,1,0:T(8,128)} async-done(((f32[4,1024,128]{2,1,0:T(8,128)}), f32[4,1024,128]{2,1,0:T(8,128)}) %all-reduce.6.cloned.1.call-update) | async-done | bytes 2097168 | tf_op jit(solution)/shard_map/psum | solution.py:10
  115.4 1.3 copy-done.4
  118.0 4.8 broadcast_in_dim.35.clone
  122.8 315.8 %while.24 = (s32[]{:T(128)}, f32[5120,4,128]{2,1,0:T(4,128)}, bf16[4,1024,5120]{2,1,0:T(8,128)(2,1)}, bf16[1,1024,128]{2,1,0:T(8,128)(2,1)S(1)}, s32[]{:T(128)}, /*index=5*/s32[]{:T(128)}, s32[]{:T(128)}) while((s32[]{:T(128)}, f32[5120,4,128]{2,1,0:T(4,128)}, bf16[4,1024,5120]{2,1,0:T(8,128)(2,1)}, bf16[1,1024,128]{2,1,0:T(8,128)(2,1)S(1)}, ...), condition=%wide.region_2.3_spmd, body=%wide.region_1.2_spmd.sunk | while | flops 1342832640 | bytes 26476668 | solution.py:19
  122.8 6.3 constant_dynamic-slice_fusion.6
  129.1 5.8 fusion.56
  134.8 66.9 %dynamic_update_slice.23 = f32[5120,4,128]{2,1,0:T(4,128)} dynamic-update-slice(f32[5120,4,128]{2,1,0:T(4,128)} %get-tuple-element.226, f32[5120,1,128]{2,1,0:T(1,128)S(1)} %bitcast.87, s32[]{:T(128)} %constant.114.clone.1..sunk, s32[]{:T(128)S(6)} %select_n.50, s32[]{:T(128)} %constant.114.clone.1..sunk) | dynamic-update-slice | bytes 5242884 | tf_op jit(solution)/shard_map/while/body/jit(dynamic_update_index_in_dim)/dynamic_update_slice | solution.py:69
  201.7 6.3 constant_dynamic-slice_fusion.6
  208.0 5.8 fusion.56
  213.8 66.9 %dynamic_update_slice.23 = f32[5120,4,128]{2,1,0:T(4,128)} dynamic-update-slice(f32[5120,4,128]{2,1,0:T(4,128)} %get-tuple-element.226, f32[5120,1,128]{2,1,0:T(1,128)S(1)} %bitcast.87, s32[]{:T(128)} %constant.114.clone.1..sunk, s32[]{:T(128)S(6)} %select_n.50, s32[]{:T(128)} %constant.114.clone.1..sunk) | dynamic-update-slice | bytes 5242884 | tf_op jit(solution)/shard_map/while/body/jit(dynamic_update_index_in_dim)/dynamic_update_slice | solution.py:69
  280.7 6.3 constant_dynamic-slice_fusion.6
  287.0 5.8 fusion.56
  292.7 66.9 %dynamic_update_slice.23 = f32[5120,4,128]{2,1,0:T(4,128)} dynamic-update-slice(f32[5120,4,128]{2,1,0:T(4,128)} %get-tuple-element.226, f32[5120,1,128]{2,1,0:T(1,128)S(1)} %bitcast.87, s32[]{:T(128)} %constant.114.clone.1..sunk, s32[]{:T(128)S(6)} %select_n.50, s32[]{:T(128)} %constant.114.clone.1..sunk) | dynamic-update-slice | bytes 5242884 | tf_op jit(solution)/shard_map/while/body/jit(dynamic_update_index_in_dim)/dynamic_update_slice | solution.py:69
  359.6 6.3 constant_dynamic-slice_fusion.6
  365.9 5.8 fusion.56
  371.7 66.9 %dynamic_update_slice.23 = f32[5120,4,128]{2,1,0:T(4,128)} dynamic-update-slice(f32[5120,4,128]{2,1,0:T(4,128)} %get-tuple-element.226, f32[5120,1,128]{2,1,0:T(1,128)S(1)} %bitcast.87, s32[]{:T(128)} %constant.114.clone.1..sunk, s32[]{:T(128)S(6)} %select_n.50, s32[]{:T(128)} %constant.114.clone.1..sunk) | dynamic-update-slice | bytes 5242884 | tf_op jit(solution)/shard_map/while/body/jit(dynamic_update_index_in_dim)/dynamic_update_slice | solution.py:69
  440.5 212.4 %all-reduce.12.cloned.1.call-done = f32[5120,4,128]{2,1,0:T(4,128)} async-done(((f32[5120,4,128]{2,1,0:T(4,128)}), f32[5120,4,128]{2,1,0:T(4,128)}) %all-reduce.12.cloned.1.call-update) | async-done | bytes 10485776
  652.9 2.5 dynamic-slice_bitcast_fusion
  655.6 56.7 %all-reduce.8.cloned.1.call-done = f32[1,640,4,128]{3,2,1,0:T(4,128)} async-done(((f32[1,640,4,128]{3,2,1,0:T(4,128)}), f32[1,640,4,128]{3,2,1,0:T(4,128)}) %all-reduce.8.cloned.1.call-update) | async-done | bytes 1310736 | tf_op jit(solution)/shard_map/psum | solution.py:10
  712.3 2.6 subtract_convert_fusion
  715.1 56.1 %all-gather.7.cloned.1.call-done = bf16[1,5120,4,128]{3,2,0,1:T(4,128)(2,1)} async-done(((bf16[1,640,4,128]{3,2,0,1:T(4,128)(2,1)}), bf16[1,5120,4,128]{3,2,0,1:T(4,128)(2,1)}) %all-gather.7.cloned.1.call-update) | async-done | bytes 5242896 | tf_op jit(solution)/shard_map/all_gather | solution.py:97
  771.1 5.5 copy.22
  776.7 24.3 %while.25 = (s32[]{:T(128)}, f32[4,1024,128]{2,1,0:T(8,128)S(1)}, s32[]{:T(128)}, bf16[4,1024,5120]{2,1,0:T(8,128)(2,1)}, bf16[5120,4,128]{2,0,1:T(8,128)(2,1)}, /*index=5*/s32[]{:T(128)}, s32[]{:T(128)}, s32[]{:T(128)}) while((s32[]{:T(128)}, f32[4,1024,128]{2,1,0:T(8,128)S(1)}, s32[]{:T(128)}, bf16[4,1024,5120]{2,1,0:T(8,128)(2,1)}, ...), condition=%wide.region_6.7_spmd, body=%wide.region_5.6_spmd.sunk | while | flops 1342308352 | bytes 13895291 | solution.py:19
  776.8 6.0 fusion.59
  782.9 6.0 fusion.59
  789.0 6.0 fusion.59
  795.1 6.0 fusion.59
  802.5 66.5 %all-reduce.10.cloned.1.call-done = f32[4,1024,128]{2,1,0:T(8,128)} async-done(((f32[4,1024,128]{2,1,0:T(8,128)}), f32[4,1024,128]{2,1,0:T(8,128)}) %all-reduce.10.cloned.1.call-update) | async-done | bytes 2097168 | tf_op jit(solution)/shard_map/psum | solution.py:10
  869.0 7.4 fusion.33
  876.5 38.0 %reduce-scatter.2.cloned.1.call-done = f32[640,128]{0,1:T(8,128)} async-done(((f32[5120,128]{0,1:T(8,128)}), f32[640,128]{0,1:T(8,128)}) %reduce-scatter.2.cloned.1.call-update) | async-done | bytes 327696 | tf_op jit(solution)/shard_map/reduce_scatter | solution.py:102
  (48 shorter events, 10.7 us)
Async XLA Ops:
  7.2 1.1 copy-start
  7.2 29.2 %all-gather.5.cloned.1.call-start = ((), (), s32[]{:S(2)}) async-start(), calls=%async_computation.5 | async-start | bytes 1474560 | tf_op jit(solution)/shard_map/all_gather | solution.py:48
  9.0 106.3 %all-reduce.6.cloned.1.call-start = ((), (), s32[]{:S(2)}) async-start(), calls=%async_computation.1 | async-start | bytes 4194304 | tf_op jit(solution)/shard_map/psum | solution.py:10
  44.6 1.6 copy-start.6
  44.8 1.3 copy-start.3
  46.1 606.8 %all-reduce.12.cloned.1.call-start = ((), (), s32[]{:S(2)}) async-start(), calls=%async_computation.7 | async-start | bytes 20971520
  115.4 1.4 copy-start.4
  438.6 0.7 copy-start.8
  438.6 216.8 %copy-start.7 = (f32[1,640,4]{1,2,0:T(4,128)S(1)}, f32[1,640,4]{1,2,0:T(4,128)}, u32[]{:S(2)}) copy-start(f32[1,640,4]{1,2,0:T(4,128)} %param.17) | copy-start | bytes 30724
  438.6 273.7 %copy-start.5 = (bf16[1,640,4,128]{3,2,1,0:T(4,128)(2,1)S(1)}, bf16[1,640,4,128]{3,2,1,0:T(4,128)(2,1)}, u32[]{:S(2)}) copy-start(bf16[1,640,4,128]{3,2,1,0:T(4,128)(2,1)} %param.16) | copy-start | bytes 1966084
  438.6 273.7 %all-reduce.8.cloned.1.call-start = ((), (), s32[]{:S(2)}) async-start(), calls=%async_computation.2 | async-start | bytes 2621440 | tf_op jit(solution)/shard_map/psum | solution.py:10
  655.4 115.8 %all-gather.7.cloned.1.call-start = ((), (), s32[]{:S(2)}) async-start(), calls=%async_computation.6 | async-start | bytes 5898240 | tf_op jit(solution)/shard_map/all_gather | solution.py:97
  715.0 154.0 %all-reduce.10.cloned.1.call-start = ((), (), s32[]{:S(2)}) async-start(), calls=%async_computation.3 | async-start | bytes 4194304 | tf_op jit(solution)/shard_map/psum | solution.py:10
  801.1 1.3 copy-start.2
  802.5 112.0 %reduce-scatter.2.cloned.1.call-start = ((), (), s32[]{:S(2)}) async-start(), calls=%async_computation.4 | async-start | bytes 2949120 | tf_op jit(solution)/shard_map/reduce_scatter | solution.py:102
  869.0 47.3 %copy-start.1 = (bf16[4,1,640,128]{3,2,1,0:T(8,128)(2,1)S(1)}, bf16[4,1,640,128]{3,2,1,0:T(8,128)(2,1)}, u32[]{:S(2)}) copy-start(bf16[4,1,640,128]{3,2,1,0:T(8,128)(2,1)} %param.11) | copy-start | bytes 1966084
Sparse Core Ops, SparseCore 0:
  10.2 26.1 all-gather.4
  46.2 68.9 all-reduce.5
  438.7 214.1 all-reduce.11
  655.8 56.4 all-reduce.7
  715.1 55.9 all-gather.6
  802.6 66.3 all-reduce.9
  876.6 37.8 reduce-scatter.1
where the time goes:
time: 930 us; the launch traced here: 923 us
  waiting for transfers between devices  526 us (57%)
  local copies, waits for them, and re-layouts  315 us (34%)
  matrix products  62.5 us (7%)
  between operations  14.9 us (2%)
    dynamic_update_slice x4, local copies, waits for them, and re-layouts, update(): return lax.dynamic_update_index_in_dim(current, before + contrib, target, 1)  268 us
    unnamed x8, waiting for transfers between devices  213 us
    psum x3, waiting for transfers between devices, over_sources(): return lax.psum(values, 'layer')  192 us
    all_gather x1, waiting for transfers between devices, per_device(): lax.all_gather(own_errors, 'lat', axis=0, tiled=True)  56.1 us
    reduce_scatter x1, waiting for transfers between devices, per_device(): lax.psum_scatter(lax.dot_general(encoder_rows, own_grad, (((0,), (0,)), (...  38 us
    all_gather x1, waiting for transfers between devices, per_device(): full_input = lax.all_gather(own_input, 'lat', axis=0, tiled=True)  27.4 us
    dynamic_slice x4, local copies, waits for them, and re-layouts, update(): before = lax.dynamic_index_in_dim(current, target, 1, keepdims=False)  25 us
    dot_general x4, matrix products, update(): contrib = jnp.dot(weights, error_rows, preferred_element_type=jnp.float32)  24 us
  transfers between devices with their start and end apart: 7, of which 7 were waited for; matrix products, arithmetic and copies ran while one was open for 0% of the time, Pallas kernels for 0%

commit v1 on v0

--- a/solution.py
+++ b/solution.py
@@ -7,7 +7,7 @@
 
 
 def over_sources(values):
-    return lax.psum(values, "layer")
+    return jnp.sum(lax.all_gather(values, "layer"), axis=0)
 
 
 def run_blocks(totals, source_row, blocks, base_target, low_target, high_target, update):

time: 930 us -> 591 us (0.64)
  local copies, waits for them, and re-layouts: 315 us -> 30 us
  waiting for transfers between devices: 526 us -> 459 us
  matrix products: 62.5 us -> 73.3 us
    dynamic_update_slice x4 -> x0, local copies, waits for them, and re-layouts: 268 us -> none  [update(): return lax.dynamic_update_index_in_dim(current, before + contrib, target, 1)]
    all_gather x0 -> x3, waiting for transfers between devices: none -> 230 us  [over_sources(): return jnp.sum(lax.all_gather(values, 'layer'), axis=0)]
    unnamed x8 -> x7, waiting for transfers between devices: 213 us -> 0.11 us
    psum x3 -> x0, waiting for transfers between devices: 192 us -> none  [over_sources(): return lax.psum(values, 'layer')]
    reduce_scatter x0 -> x1, waiting for transfers between devices: none -> 109 us  [per_device(): lax.psum_scatter(forward_term(), 'lat', scatter_dimension=0, tiled=True)]
    dynamic_slice x4, local copies, waits for them, and re-layouts: 25 us -> 7.63 us  [update(): before = lax.dynamic_index_in_dim(current, target, 1, keepdims=False)]
    reduce_sum x0 -> x3, other arithmetic: none -> 11.2 us  [over_sources(): return jnp.sum(lax.all_gather(values, 'layer'), axis=0)]
    dot_general x4, matrix products: 23 us -> 34 us  [update(): lax.dot_general(weights, latent, (((0,), (0,)), ((), ())), preferred_elem...]
  transfers between devices with their start and end apart: 7 -> 7, of which waited for: 7 -> 7; matrix products, arithmetic and copies ran while one was open for 0% -> 1% of each run, Pallas kernels for 0% -> 0%
where the time goes in v1:
time: 591 us
  waiting for transfers between devices  459 us (78%)
  matrix products  73.3 us (12%)
  local copies, waits for them, and re-layouts  30 us (5%)
  between operations  14.3 us (2%)
  other arithmetic  13.8 us (2%)
    all_gather x3, waiting for transfers between devices, over_sources(): return jnp.sum(lax.all_gather(values, 'layer'), axis=0)  230 us
    reduce_scatter x1, waiting for transfers between devices, per_device(): lax.psum_scatter(forward_term(), 'lat', scatter_dimension=0, tiled=True)  109 us
    all_gather x1, waiting for transfers between devices, per_device(): lax.all_gather(own_errors, 'lat', axis=0, tiled=True)  55.9 us
    reduce_scatter x1, waiting for transfers between devices, per_device(): lax.psum_scatter(lax.dot_general(encoder_rows, own_grad, (((0,), (0,)), (...  36.6 us
    dot_general x4, matrix products, update(): lax.dot_general(weights, latent, (((0,), (0,)), ((), ())), preferred_elem...  34 us
    all_gather x1, waiting for transfers between devices, per_device(): full_input = lax.all_gather(own_input, 'lat', axis=0, tiled=True)  27.4 us
    dot_general x4, matrix products, update(): contrib = jnp.dot(weights, error_rows, preferred_element_type=jnp.float32)  24 us
  transfers between devices with their start and end apart: 7, of which 7 were waited for; matrix products, arithmetic and copies ran while one was open for 1% of the time, Pallas kernels for 0%

profile of v1, /device:TPU:0, one launch (start us, length us, event | category | flops | bytes accessed | tf_op | source)
XLA Modules:
  0.0 590.6 jit_solution(9620101383938846342)
XLA Ops:
  9.0 27.4 %all-gather.12.cloned.1.call-done = bf16[1,1,5120,128]{3,2,1,0:T(8,128)(2,1)} async-done(((bf16[1,1,640,128]{3,2,1,0:T(8,128)(2,1)}), bf16[1,1,5120,128]{3,2,1,0:T(8,128)(2,1)}) %all-gather.12.cloned.1.call-update) | async-done | bytes 1310736 | tf_op jit(solution)/shard_map/all_gather | solution.py:48
  36.4 8.0 %fusion.45 = f32[1,1,1024,128]{2,3,1,0:T(8,128)S(1)} fusion(bf16[1,1024,5120]{2,1,0:T(8,128)(2,1)} %param.12, bf16[1,1,5120,128]{3,2,1,0:T(8,128)(2,1)} %all-gather.12.cloned.1.call-done), kind=kOutput, calls=%fused_computation.28 | convolution fusion | flops 1342177280 | bytes 12320768 | tf_op jit(solution)/shard_map/dot_general | solution.py:49
  44.8 1.4 copy-done.3
  47.0 1.5 reshape.30
  49.2 84.1 %all-gather.10.cloned.1.call-done = f32[4,4,1024,128]{3,2,1,0:T(8,128)} async-done(((f32[1,4,1024,128]{3,2,1,0:T(8,128)}), f32[4,4,1024,128]{3,2,1,0:T(8,128)}) %all-gather.10.cloned.1.call-update) | async-done | bytes 8388624 | tf_op jit(solution)/shard_map/all_gather | solution.py:10
  133.3 4.1 reduce_sum.29
  139.0 4.7 broadcast_in_dim.31
  143.7 41.7 %while.24 = (s32[]{:T(128)}, f32[5120,4,128]{2,0,1:T(8,128)}, bf16[4,1024,5120]{2,1,0:T(8,128)(2,1)}, bf16[1,1024,128]{2,1,0:T(8,128)(2,1)S(1)}, s32[]{:T(128)}, /*index=5*/s32[]{:T(128)}, s32[]{:T(128)}) while((s32[]{:T(128)}, f32[5120,4,128]{2,0,1:T(8,128)}, bf16[4,1024,5120]{2,1,0:T(8,128)(2,1)}, bf16[1,1024,128]{2,1,0:T(8,128)(2,1)S(1)}, ...), condition=%wide.region_2.3_spmd, body=%wide.region_1.2_spmd.sunk | while | flops 1342832640 | bytes 21234804 | solution.py:19
  143.7 1.9 constant_dynamic-slice_fusion.8
  145.6 8.5 %fusion.61 = f32[5120,4,128]{2,0,1:T(8,128)} fusion(f32[5120,4,128]{2,0,1:T(8,128)} %get-tuple-element.241, s32[]{:T(128)S(6)} %select_n.50, bf16[4,1024,5120]{2,1,0:T(8,128)(2,1)} %get-tuple-element.249, f32[5120,1,128]{2,0,1:T(8,128)S(1)} %constant_dynamic-slice_fusion.8, bf16[1,1024,128]{2,1,0:T(8,128)(2,1)S(1)} %get-tuple-element.250), kind=kOutput, calls=%fused_computation.5.clone.1 | convolution fusion | flops 1342832640 | bytes 15991808 | tf_op jit(solution)/shard_map/while/body/dot_general | solution.py:65
  154.1 1.9 constant_dynamic-slice_fusion.8
  156.0 8.5 %fusion.61 = f32[5120,4,128]{2,0,1:T(8,128)} fusion(f32[5120,4,128]{2,0,1:T(8,128)} %get-tuple-element.241, s32[]{:T(128)S(6)} %select_n.50, bf16[4,1024,5120]{2,1,0:T(8,128)(2,1)} %get-tuple-element.249, f32[5120,1,128]{2,0,1:T(8,128)S(1)} %constant_dynamic-slice_fusion.8, bf16[1,1024,128]{2,1,0:T(8,128)(2,1)S(1)} %get-tuple-element.250), kind=kOutput, calls=%fused_computation.5.clone.1 | convolution fusion | flops 1342832640 | bytes 15991808 | tf_op jit(solution)/shard_map/while/body/dot_general | solution.py:65
  164.5 1.9 constant_dynamic-slice_fusion.8
  166.5 8.5 %fusion.61 = f32[5120,4,128]{2,0,1:T(8,128)} fusion(f32[5120,4,128]{2,0,1:T(8,128)} %get-tuple-element.241, s32[]{:T(128)S(6)} %select_n.50, bf16[4,1024,5120]{2,1,0:T(8,128)(2,1)} %get-tuple-element.249, f32[5120,1,128]{2,0,1:T(8,128)S(1)} %constant_dynamic-slice_fusion.8, bf16[1,1024,128]{2,1,0:T(8,128)(2,1)S(1)} %get-tuple-element.250), kind=kOutput, calls=%fused_computation.5.clone.1 | convolution fusion | flops 1342832640 | bytes 15991808 | tf_op jit(solution)/shard_map/while/body/dot_general | solution.py:65
  174.9 1.9 constant_dynamic-slice_fusion.8
  176.8 8.6 %fusion.61 = f32[5120,4,128]{2,0,1:T(8,128)} fusion(f32[5120,4,128]{2,0,1:T(8,128)} %get-tuple-element.241, s32[]{:T(128)S(6)} %select_n.50, bf16[4,1024,5120]{2,1,0:T(8,128)(2,1)} %get-tuple-element.249, f32[5120,1,128]{2,0,1:T(8,128)S(1)} %constant_dynamic-slice_fusion.8, bf16[1,1024,128]{2,1,0:T(8,128)(2,1)S(1)} %get-tuple-element.250), kind=kOutput, calls=%fused_computation.5.clone.1 | convolution fusion | flops 1342832640 | bytes 15991808 | tf_op jit(solution)/shard_map/while/body/dot_general | solution.py:65
  185.5 108.5 %reduce-scatter.3.cloned.1.call-done = f32[640,4,128]{2,0,1:T(8,128)} async-done(((f32[5120,4,128]{2,0,1:T(8,128)}), f32[640,4,128]{2,0,1:T(8,128)}) %reduce-scatter.3.cloned.1.call-update) | async-done | bytes 1310736 | tf_op jit(solution)/shard_map/reduce_scatter | solution.py:75
  294.1 61.4 %all-gather.14.cloned.1.call-done = f32[2560,4,128]{2,0,1:T(8,128)} async-done(((f32[640,4,128]{2,0,1:T(8,128)}), f32[2560,4,128]{2,0,1:T(8,128)}) %all-gather.14.cloned.1.call-update) | async-done | bytes 5242896 | tf_op jit(solution)/shard_map/all_gather | solution.py:10
  355.5 3.0 reduce.1
  358.9 1.3 copy.29
  360.5 55.9 %all-gather.16.cloned.1.call-done = bf16[1,5120,4,128]{3,2,0,1:T(4,128)(2,1)} async-done(((bf16[1,640,4,128]{3,2,0,1:T(4,128)(2,1)}), bf16[1,5120,4,128]{3,2,0,1:T(4,128)(2,1)}) %all-gather.16.cloned.1.call-update) | async-done | bytes 5242896 | tf_op jit(solution)/shard_map/all_gather | solution.py:97
  416.4 5.5 copy.31
  422.0 24.3 %while.25 = (s32[]{:T(128)}, f32[4,1024,128]{2,1,0:T(8,128)S(1)}, s32[]{:T(128)}, bf16[4,1024,5120]{2,1,0:T(8,128)(2,1)}, bf16[5120,4,128]{2,0,1:T(8,128)(2,1)}, /*index=5*/s32[]{:T(128)}, s32[]{:T(128)}, s32[]{:T(128)}) while((s32[]{:T(128)}, f32[4,1024,128]{2,1,0:T(8,128)S(1)}, s32[]{:T(128)}, bf16[4,1024,5120]{2,1,0:T(8,128)(2,1)}, ...), condition=%wide.region_6.7_spmd, body=%wide.region_5.6_spmd.sunk | while | flops 1342308352 | bytes 13895291 | solution.py:19
  422.1 6.0 %fusion.64 = f32[4,1024,128]{2,1,0:T(8,128)S(1)} fusion(f32[4,1024,128]{2,1,0:T(8,128)S(1)} %get-tuple-element.263, s32[]{:T(128)} %get-tuple-element.272, bf16[5120,4,128]{2,0,1:T(8,128)(2,1)} %get-tuple-element.274, s32[]{:T(128)S(6)} %select_n.51, bf16[4,1024,5120]{2,1,0:T(8,128)(2,1)} %get-tuple-element.273, ...), kind=kOutput, calls=%fused_computation.16.clone.1 | convolution fusion | flops 1342308352 | bytes 12846592 | tf_op jit(solution)/shard_map/while/body/dot_general | solution.py:89
  428.2 6.0 %fusion.64 = f32[4,1024,128]{2,1,0:T(8,128)S(1)} fusion(f32[4,1024,128]{2,1,0:T(8,128)S(1)} %get-tuple-element.263, s32[]{:T(128)} %get-tuple-element.272, bf16[5120,4,128]{2,0,1:T(8,128)(2,1)} %get-tuple-element.274, s32[]{:T(128)S(6)} %select_n.51, bf16[4,1024,5120]{2,1,0:T(8,128)(2,1)} %get-tuple-element.273, ...), kind=kOutput, calls=%fused_computation.16.clone.1 | convolution fusion | flops 1342308352 | bytes 12846592 | tf_op jit(solution)/shard_map/while/body/dot_general | solution.py:89
  434.3 6.0 %fusion.64 = f32[4,1024,128]{2,1,0:T(8,128)S(1)} fusion(f32[4,1024,128]{2,1,0:T(8,128)S(1)} %get-tuple-element.263, s32[]{:T(128)} %get-tuple-element.272, bf16[5120,4,128]{2,0,1:T(8,128)(2,1)} %get-tuple-element.274, s32[]{:T(128)S(6)} %select_n.51, bf16[4,1024,5120]{2,1,0:T(8,128)(2,1)} %get-tuple-element.273, ...), kind=kOutput, calls=%fused_computation.16.clone.1 | convolution fusion | flops 1342308352 | bytes 12846592 | tf_op jit(solution)/shard_map/while/body/dot_general | solution.py:89
  440.4 6.0 %fusion.64 = f32[4,1024,128]{2,1,0:T(8,128)S(1)} fusion(f32[4,1024,128]{2,1,0:T(8,128)S(1)} %get-tuple-element.263, s32[]{:T(128)} %get-tuple-element.272, bf16[5120,4,128]{2,0,1:T(8,128)(2,1)} %get-tuple-element.274, s32[]{:T(128)S(6)} %select_n.51, bf16[4,1024,5120]{2,1,0:T(8,128)(2,1)} %get-tuple-element.273, ...), kind=kOutput, calls=%fused_computation.16.clone.1 | convolution fusion | flops 1342308352 | bytes 12846592 | tf_op jit(solution)/shard_map/while/body/dot_general | solution.py:89
  446.4 1.4 copy-done.2
  447.8 84.5 %all-gather.18.cloned.1.call-done = f32[16,1024,128]{2,1,0:T(8,128)} async-done(((f32[4,1024,128]{2,1,0:T(8,128)}), f32[16,1024,128]{2,1,0:T(8,128)}) %all-gather.18.cloned.1.call-update) | async-done | bytes 8388624 | tf_op jit(solution)/shard_map/all_gather | solution.py:10
  532.3 4.1 reduce_sum.32
  536.7 7.3 %fusion.39 = f32[5120,128]{0,1:T(8,128)} fusion(bf16[1,1024,5120]{2,1,0:T(8,128)(2,1)} %param.12, f32[1,1024,128]{1,2,0:T(8,128)S(1)} %copy.36, f32[4,1024,128]{1,2,0:T(8,128)} %reshape.30, s32[]{:T(128)} %select_n.47), kind=kOutput, calls=%fused_computation.23 | convolution fusion | flops 1342439424 | bytes 14156288 | tf_op jit(solution)/shard_map/dot_general | solution.py:103
  545.4 36.6 %reduce-scatter.5.cloned.1.call-done = f32[640,128]{0,1:T(8,128)} async-done(((f32[5120,128]{0,1:T(8,128)}), f32[640,128]{0,1:T(8,128)}) %reduce-scatter.5.cloned.1.call-update) | async-done | bytes 327696 | tf_op jit(solution)/shard_map/reduce_scatter | solution.py:102
  (49 shorter events, 9.8 us)
Async XLA Ops:
  7.2 1.1 copy-start
  7.2 29.2 %all-gather.12.cloned.1.call-start = ((), (), s32[]{:S(2)}) async-start(), calls=%async_computation.5 | async-start | bytes 1474560 | tf_op jit(solution)/shard_map/all_gather | solution.py:48
  9.0 124.4 %all-gather.10.cloned.1.call-start = ((), (), s32[]{:S(2)}) async-start(), calls=%async_computation.2 | async-start | bytes 10485760 | tf_op jit(solution)/shard_map/all_gather | solution.py:10
  44.6 1.7 copy-start.5
  44.8 1.4 copy-start.3
  46.2 247.8 %reduce-scatter.3.cloned.1.call-start = ((), (), s32[]{:S(2)}) async-start(), calls=%async_computation.3 | async-start | bytes 11796480 | tf_op jit(solution)/shard_map/reduce_scatter | solution.py:75
  185.4 170.1 %all-gather.14.cloned.1.call-start = ((), (), s32[]{:S(2)}) async-start(), calls=%async_computation.6 | async-start | bytes 6553600 | tf_op jit(solution)/shard_map/all_gather | solution.py:10
  294.0 122.4 %all-gather.16.cloned.1.call-start = ((), (), s32[]{:S(2)}) async-start(), calls=%async_computation.7 | async-start | bytes 5898240 | tf_op jit(solution)/shard_map/all_gather | solution.py:97
  355.5 3.0 copy-start.4
  355.5 3.0 copy-start.6
  360.3 172.1 %all-gather.18.cloned.1.call-start = ((), (), s32[]{:S(2)}) async-start(), calls=%async_computation.8 | async-start | bytes 10485760 | tf_op jit(solution)/shard_map/all_gather | solution.py:10
  446.4 1.4 copy-start.2
  447.8 134.2 %reduce-scatter.5.cloned.1.call-start = ((), (), s32[]{:S(2)}) async-start(), calls=%async_computation.4 | async-start | bytes 2949120 | tf_op jit(solution)/shard_map/reduce_scatter | solution.py:102
  536.7 47.1 %copy-start.1 = (bf16[4,1,640,128]{3,2,1,0:T(8,128)(2,1)S(1)}, bf16[4,1,640,128]{3,2,1,0:T(8,128)(2,1)}, u32[]{:S(2)}) copy-start(bf16[4,1,640,128]{3,2,1,0:T(8,128)(2,1)} %param.11) | copy-start | bytes 1966084
Sparse Core Ops, SparseCore 0:
  10.2 26.1 all-gather.11
  46.3 86.9 all-gather.9
  185.5 108.4 reduce-scatter.2
  295.7 59.7 all-gather.13
  360.4 55.9 all-gather.15
  447.9 84.4 all-gather.17
  544.1 37.7 reduce-scatter.4
